TPU v7x, 32 devices: a whole 2x2x4 slice. The times are simulated.
32 devices in a mesh: grp: 2 (over y), lat: 4 (over z), chan: 2 (over core), ens: 2 (over x).
Axes of the slice: x: 2, y: 2, z: 4, core: 2. Of those that a mesh axis runs over, the one named last changes fastest.
Arguments:
- grad_out: bfloat16 [4, 24, 48, 384], P(('grp', 'ens'), 'lat', None, 'chan'), parts along dimension 0, may hold values from -6 to 6
- pre_act: bfloat16 [4, 24, 48, 384], P(('grp', 'ens'), 'lat', None, 'chan'), parts along dimension 0, may hold values from -6 to 6
- coeffs: bfloat16 [4, 24, 24, 2, 384], P(('grp', 'ens'), ('lat', 'chan')), parts along dimension 0, may hold values from -6 to 6
- legendre: bfloat16 [24, 24, 24], P(('lat', 'chan'), None, 'ens'), may hold values from -1.25 to 1.25
- mixing: bfloat16 [384, 384], replicated, may hold values from -0.3125 to 0.3125
Outputs:
- grad_in: bfloat16 [4, 24, 48, 384], P(('grp', 'ens'), 'lat', None, 'chan'), parts along dimension 0
- mixing_grad: float32 [768, 384], P('grp'), parts along dimension 0
There are 2 independent parts, one for each index of `grp`. A program takes and returns all parts, laid end to end along the dimension named above; an argument that names none is the same for every part. Nothing has to cross between parts.
All inputs are finite; a program needn't handle non-finite values.
Results may differ from a plain program's by a relative error of at most 0.0074.
Values may be sent and summed in bfloat16 or wider, within the bound.
A program may use at most 64 MiB of HBM per device.

v0:
```python
import math
import jax
import jax.numpy as jnp
from jax import lax
from jax.sharding import PartitionSpec as P


def fourier_table(lon_count, mode_count):
    longitude = jnp.arange(lon_count, dtype=jnp.int32)[:, None]
    wavenumber = jnp.arange(mode_count, dtype=jnp.int32)[None, :]
    product_index = longitude * wavenumber % lon_count
    angles = 2.0 * math.pi / lon_count * product_index.astype(jnp.float32)
    factor = math.sqrt(2.0 / lon_count)
    stacked = jnp.stack([jnp.cos(angles), -jnp.sin(angles)], axis=2) * factor
    return stacked.reshape(lon_count, 2 * mode_count).astype(jnp.bfloat16)


def silu_backward(cotangent, preact):
    values = preact.astype(jnp.float32)
    gate_value = jax.nn.sigmoid(values)
    return (
        cotangent.astype(jnp.float32) * gate_value * (1.0 + values * (1.0 - gate_value))
    ).astype(jnp.bfloat16)


def on_device(grad_out, pre_act, coeffs, legendre, mixing):
    lat_rows = grad_out.shape[1]
    lon_count = grad_out.shape[2]
    chan_cols = grad_out.shape[3]
    mode_count = lon_count // 2
    lat_devices = lax.axis_size("lat")
    chan_count = lax.axis_size("chan")
    members = lax.axis_size("ens")
    lat_count = lat_rows * lat_devices
    channels = chan_cols * chan_count
    mode_width = 2 * mode_count // (lat_devices * chan_count)
    local_modes = mode_width // 2
    fourier = fourier_table(lon_count, mode_count)
    scaled = silu_backward(grad_out[0], pre_act[0])
    spectral = jnp.einsum(
        "nk,anc->akc", fourier, scaled, preferred_element_type=jnp.float32
    ).astype(jnp.bfloat16)
    exchanged = lax.all_to_all(
        lax.all_to_all(spectral, "lat", split_axis=1, concat_axis=0, tiled=True),
        "chan",
        split_axis=1,
        concat_axis=2,
        tiled=True,
    )
    spectral_modes = exchanged.reshape(lat_count, local_modes, 2, channels)
    legendre_full = lax.all_gather(legendre, "ens", axis=2, tiled=True)
    coef_grad = jnp.einsum(
        "mla,amrc->mlrc", legendre_full, spectral_modes, preferred_element_type=jnp.float32
    ).astype(jnp.bfloat16)
    stored = coeffs[0].reshape(-1, channels)
    flat_grad = coef_grad.reshape(-1, channels)
    weight_grad = lax.dot_general(
        stored, flat_grad, (((0,), (0,)), ((), ())), preferred_element_type=jnp.float32
    )
    weight_grad = weight_grad * (1.0 / (members * mode_count))
    weight_grad = lax.psum(weight_grad, ("lat", "chan", "ens"))
    mixed_grad = lax.dot_general(
        coef_grad, mixing, (((3,), (1,)), ((), ())), preferred_element_type=jnp.float32
    ).astype(jnp.bfloat16)
    returned = jnp.einsum(
        "mla,mlrc->amrc", legendre_full, mixed_grad, preferred_element_type=jnp.float32
    ).astype(jnp.bfloat16)
    shaped = returned.reshape(lat_count, 1, mode_width, channels)
    received = lax.all_to_all(
        lax.all_to_all(shaped, "lat", split_axis=0, concat_axis=1, tiled=True),
        "chan",
        split_axis=3,
        concat_axis=2,
        tiled=True,
    )
    row_coeffs = received.reshape(lat_rows, 2 * mode_count, chan_cols)
    spatial = jnp.einsum("nk,akc->anc", fourier, row_coeffs, preferred_element_type=jnp.float32)
    result = (grad_out[0].astype(jnp.float32) + spatial).astype(jnp.bfloat16)
    return (result[None], weight_grad)


def solution(mesh):
    placed = (
        P(("grp", "ens"), "lat", None, "chan"),
        P(("grp", "ens"), "lat", None, "chan"),
        P(("grp", "ens"), ("lat", "chan"), None, None, None),
        P(("lat", "chan"), None, "ens"),
        P(),
    )
    return jax.shard_map(
        on_device,
        mesh=mesh,
        in_specs=placed,
        out_specs=(P(("grp", "ens"), "lat", None, "chan"), P("grp", None)),
        check_vma=False,
    )
```

profile of v0, /device:TPU:0, one launch (start us, length us, event | category | flops | bytes accessed | tf_op | source)
XLA Modules:
  0.0 128.6 jit_solution(154595205387489412)
XLA Ops:
  7.2 0.0 copy-start
  7.2 0.0 copy-start.3
  7.2 0.0 copy-start.2
  7.2 0.1 sine_negate_fusion
  7.3 1.3 fusion.4
  8.6 0.7 copy.47
  9.3 6.3 %all-to-all-start = ((bf16[6,48,192]{2,0,1:T(8,128)(2,1)}), bf16[6,48,192]{2,0,1:T(8,128)(2,1)S(1)}, u32[]{:S(2)}, u32[]{:S(2)}) async-start(bf16[6,48,192]{2,0,1:T(8,128)(2,1)} %copy.47), calls=%async_computation | async-start | bytes 393216 | tf_op jit(solution)/shard_map/all_to_all | solution.py:44
  15.6 0.0 all-reduce.2.cloned.1.call-start
  15.6 0.0 copy-done.3
  15.6 0.0 copy-done.2
  15.7 4.4 %all_gather.3 = bf16[3,24,24]{1,0,2:T(4,128)(2,1)S(1)} all-gather(bf16[3,24,12]{1,0,2:T(4,128)(2,1)S(1)} %copy.51), channel_id=1, replica_groups=mesh['grp'=2,'lat'=4,'chan'=2,'ens'=2] {'ens'}, dimensions={2}, use_global_device_ids=true | all-gather | bytes 5184 | tf_op jit(solution)/shard_map/all_gather | solution.py:51
  20.1 3.0 %all-to-all-done = bf16[6,48,192]{2,0,1:T(8,128)(2,1)S(1)} async-done(((bf16[6,48,192]{2,0,1:T(8,128)(2,1)}), bf16[6,48,192]{2,0,1:T(8,128)(2,1)S(1)}, u32[]{:S(2)}, u32[]{:S(2)}) %all-to-all-start) | async-done | bytes 110624 | tf_op jit(solution)/shard_map/all_to_all | solution.py:44
  23.2 0.1 all_to_all.51
  23.3 3.8 %all_to_all.66 = bf16[24,12,192]{2,0,1:T(8,128)(2,1)S(1)} all-to-all(bf16[24,12,192]{2,0,1:T(8,128)(2,1)S(1)} %all_to_all.51), channel_id=1, replica_groups=mesh['grp'=2,'lat'=4,'chan'=2,'ens'=2] {'chan'}, dimensions={1} | all-to-all | bytes 221184 | tf_op jit(solution)/shard_map/all_to_all | solution.py:43
  27.1 0.1 copy.50
  27.2 0.1 reshape.90
  27.3 0.2 fusion.5
  27.6 0.1 copy.60
  27.7 1.1 fusion
  28.8 0.0 all-reduce.2.cloned.1.call-update
  28.9 0.0 copy-done
  28.9 0.4 convolution_convert_fusion.1
  29.3 9.9 %all_to_all.67 = bf16[24,1,6,384]{3,2,1,0:T(8,128)(2,1)S(1)} all-to-all(bf16[24,1,6,384]{3,2,1,0:T(8,128)(2,1)S(1)} %copy.54), channel_id=1, replica_groups=mesh['grp'=2,'lat'=4,'chan'=2,'ens'=2] {'lat'}, dimensions={0} | all-to-all | bytes 221184 | tf_op jit(solution)/shard_map/all_to_all | solution.py:70
  39.3 1.5 %copy.56 = bf16[6,4,6,384]{0,1,2,3:T(4,128)(2,1)S(1)} copy(bf16[6,4,6,384]{3,2,0,1:T(8,128)(2,1)S(1)} %bitcast.68) | data formatting | bytes 221184 | tf_op jit(solution)/shard_map/all_to_all | solution.py:70
  40.7 4.1 %reshape.100 = bf16[2,2,13824]{2,1,0:T(2,128)(2,1)S(1)} reshape(bf16[384,6,4,6]{3,2,1,0:T(4,128)(2,1)S(1)} %bitcast.65) | data formatting | bytes 221184
  44.8 3.8 %all_to_all.68 = bf16[2,2,13824]{2,1,0:T(2,128)(2,1)S(1)} all-to-all(bf16[2,2,13824]{2,1,0:T(2,128)(2,1)S(1)} %reshape.100), channel_id=1, replica_groups=mesh['grp'=2,'lat'=4,'chan'=2,'ens'=2] {'chan'}, dimensions={0} | all-to-all | bytes 221184 | tf_op jit(solution)/shard_map/all_to_all | solution.py:69
  48.7 0.0 copy-start.1
  48.7 5.4 %reshape.101 = bf16[384,6,4,6]{3,2,1,0:T(4,128)(2,1)S(1)} reshape(bf16[2,2,13824]{2,1,0:T(2,128)(2,1)S(1)} %all_to_all.68) | data formatting | bytes 221184
  54.0 2.5 %copy.74 = bf16[6,4,6,2,192]{4,3,1,2,0:T(2,128)(2,1)S(1)} copy(bf16[6,4,6,2,192]{0,1,2,4,3:T(4,128)(2,1)S(1)} %bitcast.66) | data formatting | bytes 221184 | tf_op jit(solution)/shard_map/all_to_all | solution.py:69
  56.6 0.1 reshape.92
  56.7 0.0 copy-done.1
  56.7 0.9 fusion.3
  57.6 62.1 %all-reduce.2.cloned.1.call-done = f32[384,384]{0,1:T(8,128)} async-done(((f32[384,384]{0,1:T(8,128)}), f32[384,384]{0,1:T(8,128)}) %all-reduce.2.cloned.1.call-update) | async-done | bytes 589840 | tf_op jit(solution)/shard_map/psum | solution.py:61
  119.7 2.1 %copy.61 = f32[384,384]{1,0:T(8,128)} copy(f32[384,384]{0,1:T(8,128)} %all-reduce.2.cloned.1.call-done) | data formatting | bytes 1179648
  (8 shorter events, 0.2 us)
Async XLA Ops:
  7.2 21.7 %copy-start = (bf16[384,384]{1,0:T(8,128)(2,1)S(1)}, bf16[384,384]{1,0:T(8,128)(2,1)}, u32[]{:S(2)}) copy-start(bf16[384,384]{1,0:T(8,128)(2,1)} %param.9) | copy-start | bytes 884740
  7.2 8.4 %copy-start.3 = (bf16[3,24,12]{1,2,0:T(8,128)(2,1)S(1)}, bf16[3,24,12]{1,2,0:T(8,128)(2,1)}, u32[]{:S(2)}) copy-start(bf16[3,24,12]{1,2,0:T(8,128)(2,1)} %param.8) | copy-start | bytes 5188
  7.2 8.4 %copy-start.2 = (bf16[1,3,24,2,384]{4,3,2,1,0:T(2,128)(2,1)S(1)}, bf16[1,3,24,2,384]{4,3,2,1,0:T(2,128)(2,1)}, u32[]{:S(2)}) copy-start(bf16[1,3,24,2,384]{4,3,2,1,0:T(2,128)(2,1)} %param.7) | copy-start | bytes 331780
  9.3 13.8 %all-to-all-start = ((bf16[6,48,192]{2,0,1:T(8,128)(2,1)}), bf16[6,48,192]{2,0,1:T(8,128)(2,1)S(1)}, u32[]{:S(2)}, u32[]{:S(2)}) async-start(bf16[6,48,192]{2,0,1:T(8,128)(2,1)} %copy.47), calls=%async_computation | async-start | bytes 393216 | tf_op jit(solution)/shard_map/all_to_all | solution.py:44
  15.6 104.0 %all-reduce.2.cloned.1.call-start = ((), (), s32[]{:S(2)}) async-start(), calls=%async_computation.4 | async-start | bytes 1179648 | tf_op jit(solution)/shard_map/psum | solution.py:61
  48.7 8.0 %copy-start.1 = (bf16[1,6,48,192]{3,2,1,0:T(8,128)(2,1)S(1)}, bf16[1,6,48,192]{3,2,1,0:T(8,128)(2,1)}, u32[]{:S(2)}) copy-start(bf16[1,6,48,192]{3,2,1,0:T(8,128)(2,1)} %param.5) | copy-start | bytes 331780
Sparse Core Ops, SparseCore 0:
  29.0 90.6 all-reduce.1
where the time goes:
time: 129 us
  waiting for transfers between devices  65.2 us (51%)
  blocking collectives  22 us (17%)
  local copies, waits for them, and re-layouts  17 us (13%)
  between operations  14.2 us (11%)
  starting transfers between devices  6.32 us (5%)
  matrix products  3.94 us (3%)
    psum x1, waiting for transfers between devices, on_device(): weight_grad = lax.psum(weight_grad, ('lat', 'chan', 'ens'))  62.1 us
    unnamed x12, local copies, waits for them, and re-layouts  11.6 us
    all_to_all x1, blocking collectives, on_device(): lax.all_to_all(shaped, 'lat', split_axis=0, concat_axis=1, tiled=True)  9.92 us
    all_to_all x1, starting transfers between devices, on_device(): lax.all_to_all(spectral, 'lat', split_axis=1, concat_axis=0, tiled=True)  6.32 us
    all_gather x1, blocking collectives, on_device(): legendre_full = lax.all_gather(legendre, 'ens', axis=2, tiled=True)  4.4 us
    all_to_all x1, blocking collectives, on_device(): lax.all_to_all(lax.all_to_all(spectral, 'lat', split_axis=1, concat_axis=...  3.82 us
    all_to_all x1, blocking collectives, on_device(): lax.all_to_all(lax.all_to_all(shaped, 'lat', split_axis=0, concat_axis=1,...  3.81 us
    all_to_all x1, waiting for transfers between devices, on_device(): lax.all_to_all(spectral, 'lat', split_axis=1, concat_axis=0, tiled=True)  3.04 us
  transfers between devices with their start and end apart: 2, of which 2 were waited for; matrix products, arithmetic and copies ran while one was open for 12% of the time, Pallas kernels for 0%

commit v1 on v0

--- a/solution.py
+++ b/solution.py
@@ -58,7 +58,7 @@
         stored, flat_grad, (((0,), (0,)), ((), ())), preferred_element_type=jnp.float32
     )
     weight_grad = weight_grad * (1.0 / (members * mode_count))
-    weight_grad = lax.psum(weight_grad, ("lat", "chan", "ens"))
+    weight_grad = lax.psum(lax.psum(weight_grad, ("chan", "ens")), "lat")
     mixed_grad = lax.dot_general(
         coef_grad, mixing, (((3,), (1,)), ((), ())), preferred_element_type=jnp.float32
     ).astype(jnp.bfloat16)

time: 129 us -> 112 us (0.87)
  waiting for transfers between devices: 65.2 us -> 47.3 us
    psum x1 -> x2, waiting for transfers between devices: 62.1 us -> 44.2 us  [on_device(): weight_grad = lax.psum(lax.psum(weight_grad, ('chan', 'ens')), 'lat')]
  transfers between devices with their start and end apart: 2 -> 3, of which waited for: 2 -> 3; matrix products, arithmetic and copies ran while one was open for 12% -> 13% of each run, Pallas kernels for 0% -> 0%
where the time goes in v1:
time: 112 us
  waiting for transfers between devices  47.3 us (42%)
  blocking collectives  23.1 us (21%)
  local copies, waits for them, and re-layouts  17 us (15%)
  between operations  14.2 us (13%)
  starting transfers between devices  6.36 us (6%)
  matrix products  3.94 us (4%)
    psum x2, waiting for transfers between devices, on_device(): weight_grad = lax.psum(lax.psum(weight_grad, ('chan', 'ens')), 'lat')  44.2 us
    unnamed x12, local copies, waits for them, and re-layouts  11.6 us
    all_to_all x1, blocking collectives, on_device(): lax.all_to_all(shaped, 'lat', split_axis=0, concat_axis=1, tiled=True)  11.1 us
    all_to_all x1, starting transfers between devices, on_device(): lax.all_to_all(spectral, 'lat', split_axis=1, concat_axis=0, tiled=True)  6.32 us
    all_gather x1, blocking collectives, on_device(): legendre_full = lax.all_gather(legendre, 'ens', axis=2, tiled=True)  4.4 us
    all_to_all x1, blocking collectives, on_device(): lax.all_to_all(lax.all_to_all(spectral, 'lat', split_axis=1, concat_axis=...  3.82 us
    all_to_all x1, blocking collectives, on_device(): lax.all_to_all(lax.all_to_all(shaped, 'lat', split_axis=0, concat_axis=1,...  3.81 us
    all_to_all x1, waiting for transfers between devices, on_device(): lax.all_to_all(spectral, 'lat', split_axis=1, concat_axis=0, tiled=True)  3.04 us
  transfers between devices with their start and end apart: 3, of which 3 were waited for; matrix products, arithmetic and copies ran while one was open for 13% of the time, Pallas kernels for 0%

profile of v1, /device:TPU:0, one launch (start us, length us, event | category | flops | bytes accessed | tf_op | source)
XLA Modules:
  0.0 111.9 jit_solution(13615211239786136773)
XLA Ops:
  7.2 0.0 copy-start
  7.2 0.0 copy-start.3
  7.2 0.0 copy-start.2
  7.2 0.1 sine_negate_fusion
  7.3 1.3 %fusion.4 = bf16[6,48,192]{2,1,0:T(8,128)(2,1)S(1)} fusion(bf16[48,48,1]{0,1,2:T(8,128)(2,1)S(1)} %bitcast.74, bf16[1,6,48,192]{3,2,1,0:T(8,128)(2,1)} %param.6, bf16[1,6,48,192]{3,2,1,0:T(8,128)(2,1)} %param.5), kind=kOutput, calls=%fused_computation.10 | convolution fusion | flops 5971968 | bytes 336384 | tf_op jit(solution)/shard_map/nk,anc->akc/dot_general | solution.py:40
  8.6 0.7 copy.47
  9.3 6.3 %all-to-all-start = ((bf16[6,48,192]{2,0,1:T(8,128)(2,1)}), bf16[6,48,192]{2,0,1:T(8,128)(2,1)S(1)}, u32[]{:S(2)}, u32[]{:S(2)}) async-start(bf16[6,48,192]{2,0,1:T(8,128)(2,1)} %copy.47), calls=%async_computation | async-start | bytes 393216 | tf_op jit(solution)/shard_map/all_to_all | solution.py:44
  15.6 0.0 all-reduce.3.cloned.1.call-start
  15.6 0.0 copy-done.3
  15.6 0.0 copy-done.2
  15.7 4.4 %all_gather.3 = bf16[3,24,24]{1,0,2:T(4,128)(2,1)S(1)} all-gather(bf16[3,24,12]{1,0,2:T(4,128)(2,1)S(1)} %copy.51), channel_id=1, replica_groups=mesh['grp'=2,'lat'=4,'chan'=2,'ens'=2] {'ens'}, dimensions={2}, use_global_device_ids=true | all-gather | bytes 5184 | tf_op jit(solution)/shard_map/all_gather | solution.py:51
  20.1 3.0 %all-to-all-done = bf16[6,48,192]{2,0,1:T(8,128)(2,1)S(1)} async-done(((bf16[6,48,192]{2,0,1:T(8,128)(2,1)}), bf16[6,48,192]{2,0,1:T(8,128)(2,1)S(1)}, u32[]{:S(2)}, u32[]{:S(2)}) %all-to-all-start) | async-done | bytes 110624 | tf_op jit(solution)/shard_map/all_to_all | solution.py:44
  23.2 0.1 all_to_all.51
  23.3 3.8 %all_to_all.66 = bf16[24,12,192]{2,0,1:T(8,128)(2,1)S(1)} all-to-all(bf16[24,12,192]{2,0,1:T(8,128)(2,1)S(1)} %all_to_all.51), channel_id=1, replica_groups=mesh['grp'=2,'lat'=4,'chan'=2,'ens'=2] {'chan'}, dimensions={1} | all-to-all | bytes 221184 | tf_op jit(solution)/shard_map/all_to_all | solution.py:43
  27.1 0.1 copy.50
  27.2 0.1 reshape.90
  27.3 0.2 fusion.5
  27.6 0.1 copy.60
  27.7 1.1 %fusion = f32[384,384]{0,1:T(8,128)} fusion(bf16[144,384]{1,0:T(8,128)(2,1)S(1)} %reshape.93, bf16[144,384]{1,0:T(8,128)(2,1)S(1)} %reshape_squeeze.3), kind=kOutput, calls=%fused_computation.1 | convolution fusion | flops 42614784 | bytes 811008 | tf_op jit(solution)/shard_map/dot_general | solution.py:57
  28.8 0.0 all-reduce.3.cloned.1.call-update
  28.9 0.0 all-reduce.5.cloned.1.call-start
  28.9 32.6 %all-reduce.3.cloned.1.call-done = f32[384,384]{0,1:T(8,128)} async-done(((f32[384,384]{0,1:T(8,128)}), f32[384,384]{0,1:T(8,128)}) %all-reduce.3.cloned.1.call-update) | async-done | bytes 589840 | tf_op jit(solution)/shard_map/psum | solution.py:61
  61.5 0.0 all-reduce.5.cloned.1.call-update
  61.5 0.0 copy-done
  61.6 0.4 convolution_convert_fusion.1
  62.0 11.1 %all_to_all.67 = bf16[24,1,6,384]{3,2,1,0:T(8,128)(2,1)S(1)} all-to-all(bf16[24,1,6,384]{3,2,1,0:T(8,128)(2,1)S(1)} %copy.54), channel_id=1, replica_groups=mesh['grp'=2,'lat'=4,'chan'=2,'ens'=2] {'lat'}, dimensions={0} | all-to-all | bytes 221184 | tf_op jit(solution)/shard_map/all_to_all | solution.py:70
  73.1 1.5 %copy.56 = bf16[6,4,6,384]{0,1,2,3:T(4,128)(2,1)S(1)} copy(bf16[6,4,6,384]{3,2,0,1:T(8,128)(2,1)S(1)} %bitcast.68) | data formatting | bytes 221184 | tf_op jit(solution)/shard_map/all_to_all | solution.py:70
  74.6 4.1 %reshape.100 = bf16[2,2,13824]{2,1,0:T(2,128)(2,1)S(1)} reshape(bf16[384,6,4,6]{3,2,1,0:T(4,128)(2,1)S(1)} %bitcast.65) | data formatting | bytes 221184
  78.7 3.8 %all_to_all.68 = bf16[2,2,13824]{2,1,0:T(2,128)(2,1)S(1)} all-to-all(bf16[2,2,13824]{2,1,0:T(2,128)(2,1)S(1)} %reshape.100), channel_id=1, replica_groups=mesh['grp'=2,'lat'=4,'chan'=2,'ens'=2] {'chan'}, dimensions={0} | all-to-all | bytes 221184 | tf_op jit(solution)/shard_map/all_to_all | solution.py:69
  82.5 0.0 copy-start.1
  82.5 5.4 %reshape.101 = bf16[384,6,4,6]{3,2,1,0:T(4,128)(2,1)S(1)} reshape(bf16[2,2,13824]{2,1,0:T(2,128)(2,1)S(1)} %all_to_all.68) | data formatting | bytes 221184
  87.9 2.5 %copy.74 = bf16[6,4,6,2,192]{4,3,1,2,0:T(2,128)(2,1)S(1)} copy(bf16[6,4,6,2,192]{0,1,2,4,3:T(4,128)(2,1)S(1)} %bitcast.66) | data formatting | bytes 221184 | tf_op jit(solution)/shard_map/all_to_all | solution.py:69
  90.4 0.1 reshape.92
  90.5 0.0 copy-done.1
  90.5 0.9 fusion.3
  91.4 11.6 %all-reduce.5.cloned.1.call-done = f32[384,384]{0,1:T(8,128)} async-done(((f32[384,384]{0,1:T(8,128)}), f32[384,384]{0,1:T(8,128)}) %all-reduce.5.cloned.1.call-update) | async-done | bytes 589840 | tf_op jit(solution)/shard_map/psum | solution.py:61
  103.0 2.1 %copy.61 = f32[384,384]{1,0:T(8,128)} copy(f32[384,384]{0,1:T(8,128)} %all-reduce.5.cloned.1.call-done) | data formatting | bytes 1179648
  (8 shorter events, 0.2 us)
Async XLA Ops:
  7.2 54.4 %copy-start = (bf16[384,384]{1,0:T(8,128)(2,1)S(1)}, bf16[384,384]{1,0:T(8,128)(2,1)}, u32[]{:S(2)}) copy-start(bf16[384,384]{1,0:T(8,128)(2,1)} %param.9) | copy-start | bytes 884740
  7.2 8.4 %copy-start.3 = (bf16[3,24,12]{1,2,0:T(8,128)(2,1)S(1)}, bf16[3,24,12]{1,2,0:T(8,128)(2,1)}, u32[]{:S(2)}) copy-start(bf16[3,24,12]{1,2,0:T(8,128)(2,1)} %param.8) | copy-start | bytes 5188
  7.2 8.4 %copy-start.2 = (bf16[1,3,24,2,384]{4,3,2,1,0:T(2,128)(2,1)S(1)}, bf16[1,3,24,2,384]{4,3,2,1,0:T(2,128)(2,1)}, u32[]{:S(2)}) copy-start(bf16[1,3,24,2,384]{4,3,2,1,0:T(2,128)(2,1)} %param.7) | copy-start | bytes 331780
  9.3 13.8 %all-to-all-start = ((bf16[6,48,192]{2,0,1:T(8,128)(2,1)}), bf16[6,48,192]{2,0,1:T(8,128)(2,1)S(1)}, u32[]{:S(2)}, u32[]{:S(2)}) async-start(bf16[6,48,192]{2,0,1:T(8,128)(2,1)} %copy.47), calls=%async_computation | async-start | bytes 393216 | tf_op jit(solution)/shard_map/all_to_all | solution.py:44
  15.6 45.9 %all-reduce.3.cloned.1.call-start = ((), (), s32[]{:S(2)}) async-start(), calls=%async_computation.4 | async-start | bytes 1179648 | tf_op jit(solution)/shard_map/psum | solution.py:61
  28.9 74.1 %all-reduce.5.cloned.1.call-start = ((), (), s32[]{:S(2)}) async-start(), calls=%async_computation.5 | async-start | bytes 1179648 | tf_op jit(solution)/shard_map/psum | solution.py:61
  82.5 8.0 %copy-start.1 = (bf16[1,6,48,192]{3,2,1,0:T(8,128)(2,1)S(1)}, bf16[1,6,48,192]{3,2,1,0:T(8,128)(2,1)}, u32[]{:S(2)}) copy-start(bf16[1,6,48,192]{3,2,1,0:T(8,128)(2,1)} %param.5) | copy-start | bytes 331780
Sparse Core Ops, SparseCore 0:
  29.0 32.4 all-reduce.2
  63.9 39.0 all-reduce.4
